TPU v7x, 512 devices: a whole 4x4x16 slice. The times are simulated.
512 devices in a mesh: blk: 8 (over z_lo), stripe: 64 (over y, x, z_hi, core).
Axes of the slice: x: 4, y: 4, z: 16 (z_hi: 2, z_lo: 8; z = z_hi * 8 + z_lo), core: 2. Of those that a mesh axis runs over, the one named last changes fastest.
Arguments:
- points: bfloat16 [262144, 64], P(('blk', 'stripe')), may hold values from -6 to 6
- coefficients: float32 [262144], P(('blk', 'stripe')), may hold values from -0.0234375 to 0.0234375
- velocity: float32 [262144], P(('blk', 'stripe')), may hold values from -0.0234375 to 0.0234375
- targets: float32 [262144], P(('blk', 'stripe')), may hold values from -6 to 6
- batch_rows: int32 [32768], P(('blk', 'stripe')), may hold values from 0 to 511
- counts: int32 [8, 64], P('blk', 'stripe'), may hold values from 1 to 64, 2048 in all within a row
Outputs:
- new_coefficients: float32 [262144], P(('blk', 'stripe'))
- new_velocity: float32 [262144], P(('blk', 'stripe'))
Inputs may be any that keep to these rules, and one draw needn't show every extreme that they name: In every index of blk, the counts of its 64 devices sum to exactly 2048, and some device's count is exactly 64. Only the first count entries of a device's slots are live. `batch_rows`: every entry, live or not, indexes the points of the device that holds it; rows may repeat.
All inputs are finite; a program needn't handle non-finite values.
Results may differ from a plain program's by a relative error of at most 0.0003.
Values may be sent and summed in bfloat16 or wider, within the bound.
A program may use at most 64 MiB of HBM per device.

v0:
```python
import math
import jax
import jax.numpy as jnp
from jax import lax
from jax.sharding import PartitionSpec as P

MOMENTUM = 0.9
STEP_SIZE = 1.0
NOISE_VAR = 8.0
KERNEL_RATE = 3.0**0.5 / 6.0


def matern_sums(row_feats, row_sq, col_points, col_coef):
    col_sq = jnp.sum(jnp.square(col_points.astype(jnp.float32)), axis=1)
    inner_prod = lax.dot_general(
        row_feats, col_points, (((1,), (1,)), ((), ())), preferred_element_type=jnp.float32
    )
    distance = jnp.sqrt(jnp.maximum(row_sq[:, None] + col_sq[None, :] - 2.0 * inner_prod, 0.0))
    scaled = KERNEL_RATE * distance
    kernel_tile = (1.0 + scaled) * jnp.exp(-scaled)
    return jnp.sum(kernel_tile * col_coef[None, :], axis=1)


def column_sums(row_feats, points, preview):
    row_sq = jnp.sum(jnp.square(row_feats.astype(jnp.float32)), axis=1)
    every_coef = lax.all_gather(preview, "blk", axis=0, tiled=True)
    zeros_init = jnp.zeros((row_feats.shape[0],), jnp.float32)
    piece_points = lax.all_gather(points, "blk", axis=0, tiled=True)
    piece_len = piece_points.shape[0]
    block_len = math.gcd(piece_len, 512)
    point_blocks = piece_points.reshape(-1, block_len, piece_points.shape[1])
    coef_blocks = every_coef.reshape(-1, block_len)

    def advance(partial_sum, column_block):
        return (
            partial_sum + matern_sums(row_feats, row_sq, column_block[0], column_block[1]),
            None,
        )

    result, unused = lax.scan(advance, zeros_init, (point_blocks, coef_blocks))
    return result


def per_device(points, coefficients, velocity, targets, batch_rows, counts):
    preview = coefficients + MOMENTUM * velocity
    slot_total = batch_rows.shape[0]
    local_size = points.shape[0]
    slot_ids = jnp.arange(slot_total, dtype=jnp.int32)
    count_here = counts.reshape((1,))
    in_count = slot_ids < count_here[0]
    picked = jnp.take(points, batch_rows, axis=0)
    group_rows = lax.all_gather(picked, "stripe", axis=0, tiled=True)
    partial_value = column_sums(group_rows, points, preview)
    kernel_rows = lax.psum_scatter(partial_value, "stripe", scatter_dimension=0, tiled=True)
    residual = jnp.where(
        in_count,
        kernel_rows + NOISE_VAR * jnp.take(preview, batch_rows) - jnp.take(targets, batch_rows),
        0.0,
    )
    scatter_rows = (batch_rows[:, None] == jnp.arange(local_size, dtype=jnp.int32)[None, :]).astype(
        jnp.float32
    )
    update_sum = jnp.dot(residual, scatter_rows, precision=lax.Precision.HIGHEST)
    new_velocity = MOMENTUM * velocity - STEP_SIZE * update_sum
    new_coefficients = coefficients + new_velocity
    return (new_coefficients, new_velocity)


def solution(mesh):
    in_specs = (
        P(("blk", "stripe"), None),
        P(("blk", "stripe")),
        P(("blk", "stripe")),
        P(("blk", "stripe")),
        P(("blk", "stripe")),
        P("blk", "stripe"),
    )
    out_specs = (P(("blk", "stripe")), P(("blk", "stripe")))
    return jax.shard_map(
        per_device, mesh=mesh, in_specs=in_specs, out_specs=out_specs, check_vma=False
    )
```

profile of v0, /device:TPU:0, one launch (start us, length us, event | category | flops | bytes accessed | tf_op | source)
XLA Modules:
  0.0 868.9 jit_solution(8727007130608261097)
XLA Ops:
  0.6 0.0 copy-start
  0.6 0.0 copy-start.1
  1.3 1.3 dynamic-slice
  3.3 0.7 compare_and_fusion
  3.9 0.7 compare_select_fusion
  4.6 0.7 multiply_add_fusion
  5.3 0.0 copy-done
  5.3 0.8 gather_fusion.2
  6.1 0.8 gather_fusion.1
  6.9 42.5 %all-gather = f32[8,1,512]{2,1,0:T(1,128)S(1)} all-gather(f32[1,1,512]{2,1,0:T(1,128)S(1)} %bitcast.38), channel_id=1, replica_groups=mesh['blk'=8,'stripe'=64] {'blk'}, dimensions={0}, use_global_device_ids=true | all-gather | bytes 18432 | tf_op jit(solution)/shard_map/all_gather | solution.py:26
  49.4 0.0 copy-done.1
  49.4 0.1 copy.12
  49.6 0.6 gather_fusion
  50.2 0.1 broadcast_select_fusion
  50.3 48.0 %all_gather.10 = bf16[4096,64]{0,1:T(8,128)(2,1)S(1)} all-gather(bf16[512,64]{0,1:T(8,128)(2,1)S(1)} %copy-done.1), channel_id=1, replica_groups=mesh['blk'=8,'stripe'=64] {'blk'}, dimensions={0}, use_global_device_ids=true | all-gather | bytes 589824 | tf_op jit(solution)/shard_map/all_gather | solution.py:28
  98.3 0.5 copy.13
  98.8 165.0 %all_gather.9 = bf16[4096,64]{1,0:T(8,128)(2,1)S(1)} all-gather(bf16[64,64]{1,0:T(8,128)(2,1)S(1)} %broadcast_select_fusion), channel_id=1, replica_groups=mesh['blk'=8,'stripe'=64] {'stripe'}, dimensions={0}, use_global_device_ids=true | all-gather | bytes 532480 | tf_op jit(solution)/shard_map/all_gather | solution.py:52
  263.8 0.6 multiply_reduce_fusion.2
  264.5 0.0 copy-start.4
  264.5 0.0 copy-start.2
  264.5 0.0 copy-start.3
  264.5 49.6 %while.11 = (s32[]{:T(128)}, f32[4096]{0:T(1024)S(1)}, f32[4096]{0:T(1024)S(1)}, bf16[8,512,64]{2,1,0:T(8,128)(2,1)S(1)}, bf16[4096,64]{1,0:T(8,128)(2,1)S(1)}, /*index=5*/f32[8,512]{1,0:T(8,128)S(1)}, s32[]{:T(128)}, s32[]{:T(128)}) while((s32[]{:T(128)}, f32[4096]{0:T(1024)S(1)}, f32[4096]{0:T(1024)S(1)}, ...), condition=%wide.region_4.5_spmd.clone, body=%wide.region_1.0_spmd.clone.sunk | while | flops 289508864 | bytes 1337459 | solution.py:40
  264.5 0.2 multiply_reduce_fusion.5
  264.7 6.0 multiply_reduce_fusion.6
  270.7 0.2 multiply_reduce_fusion.5
  270.9 6.0 multiply_reduce_fusion.6
  276.9 0.2 multiply_reduce_fusion.5
  277.1 6.0 multiply_reduce_fusion.6
  283.1 0.2 multiply_reduce_fusion.5
  283.3 6.0 multiply_reduce_fusion.6
  289.3 0.2 multiply_reduce_fusion.5
  289.5 6.0 multiply_reduce_fusion.6
  295.5 0.2 multiply_reduce_fusion.5
  295.7 6.0 multiply_reduce_fusion.6
  301.7 0.2 multiply_reduce_fusion.5
  301.9 6.0 multiply_reduce_fusion.6
  307.9 0.2 multiply_reduce_fusion.5
  308.1 6.0 multiply_reduce_fusion.6
  314.1 554.0 %all-reduce = f32[4096]{0:T(1024)S(1)} all-reduce(f32[4096]{0:T(1024)S(1)} %get-tuple-element.35), channel_id=2, replica_groups=mesh['blk'=8,'stripe'=64] {'stripe'}, use_global_device_ids=true, to_apply=%region_5.6.clone | all-reduce | flops 4096 | bytes 32768
  868.1 0.0 copy-done.4
  868.1 0.2 fusion.6
  868.3 0.0 copy-done.2
  868.3 0.0 copy-done.3
  868.3 0.6 fusion.21
  (19 shorter events, 0.1 us)
Async XLA Ops:
  0.6 4.7 copy-start
  0.6 48.8 %copy-start.1 = (bf16[512,64]{0,1:T(8,128)(2,1)S(1)}, bf16[512,64]{0,1:T(8,128)(2,1)}, u32[]{:S(2)}) copy-start(bf16[512,64]{0,1:T(8,128)(2,1)} %param.10) | copy-start | bytes 196612
  264.5 603.6 %copy-start.4 = (s32[64]{0:T(128)S(1)}, s32[64]{0:T(128)}, u32[]{:S(2)}) copy-start(s32[64]{0:T(128)} %param.14) | copy-start | bytes 772
  264.5 603.9 %copy-start.2 = (f32[512]{0:T(512)S(1)}, f32[512]{0:T(512)}, u32[]{:S(2)}) copy-start(f32[512]{0:T(512)} %param.11) | copy-start | bytes 6148
  264.5 603.8 %copy-start.3 = (f32[512]{0:T(512)S(1)}, f32[512]{0:T(512)}, u32[]{:S(2)}) copy-start(f32[512]{0:T(512)} %param.12) | copy-start | bytes 6148
where the time goes:
time: 869 us
  blocking collectives  810 us (93%)
  matrix products  48.1 us (6%)
    unnamed x1, blocking collectives  554 us
    all_gather x1, blocking collectives, per_device(): group_rows = lax.all_gather(picked, 'stripe', axis=0, tiled=True)  165 us
    all_gather x1, blocking collectives, column_sums(): piece_points = lax.all_gather(points, 'blk', axis=0, tiled=True)  48 us
    dot_general x8, matrix products, matern_sums(): lax.dot_general(row_feats, col_points, (((1,), (1,)), ((), ())), preferre...  47.9 us
    all_gather x1, blocking collectives, column_sums(): every_coef = lax.all_gather(preview, 'blk', axis=0, tiled=True)  42.5 us

commit v1 on v0

--- a/solution.py
+++ b/solution.py
@@ -23,7 +23,9 @@
 
 def column_sums(row_feats, points, preview):
     row_sq = jnp.sum(jnp.square(row_feats.astype(jnp.float32)), axis=1)
-    every_coef = lax.all_gather(preview, "blk", axis=0, tiled=True)
+    every_coef = jnp.concatenate(
+        lax.all_to_all(jnp.stack([preview] * lax.axis_size("blk")), "blk", 0, 0), axis=0
+    )
     zeros_init = jnp.zeros((row_feats.shape[0],), jnp.float32)
     piece_points = lax.all_gather(points, "blk", axis=0, tiled=True)
     piece_len = piece_points.shape[0]

time: 869 us -> 838 us (0.964)
  blocking collectives: 810 us -> 766 us
    all_gather x1 -> x0, blocking collectives: 42.5 us -> none  [column_sums(): every_coef = lax.all_gather(preview, 'blk', axis=0, tiled=True)]
  transfers between devices with their start and end apart: 0 -> 1, of which waited for: 0 -> 0; matrix products, arithmetic and copies ran while one was open for 0% -> 1% of each run, Pallas kernels for 0% -> 0%
where the time goes in v1:
time: 838 us; the launch traced here: 834 us
  blocking collectives  766 us (91%)
  matrix products  48.2 us (6%)
    unnamed x1, blocking collectives  556 us
    all_gather x1, blocking collectives, per_device(): group_rows = lax.all_gather(picked, 'stripe', axis=0, tiled=True)  162 us
    all_gather x1, blocking collectives, column_sums(): piece_points = lax.all_gather(points, 'blk', axis=0, tiled=True)  48.5 us
    dot_general x8, matrix products, matern_sums(): lax.dot_general(row_feats, col_points, (((1,), (1,)), ((), ())), preferre...  48 us
  transfers between devices with their start and end apart: 1, of which 0 were waited for; matrix products, arithmetic and copies ran while one was open for 1% of the time, Pallas kernels for 0%

profile of v1, /device:TPU:0, one launch (start us, length us, event | category | flops | bytes accessed | tf_op | source)
XLA Modules:
  0.0 834.4 jit_solution(18284601904768405946)
XLA Ops:
  0.6 0.0 copy-start
  0.6 0.7 multiply_add_fusion
  1.4 0.6 stack.2
  2.0 7.2 all-to-all-start
  9.1 0.7 compare_and_fusion
  9.8 0.7 compare_select_fusion
  10.4 1.0 copy.12
  11.4 48.5 %all_gather.7 = bf16[4096,64]{0,1:T(8,128)(2,1)S(1)} all-gather(bf16[512,64]{0,1:T(8,128)(2,1)} %param.10), channel_id=1, replica_groups=mesh['blk'=8,'stripe'=64] {'blk'}, dimensions={0}, use_global_device_ids=true | all-gather | bytes 589824 | tf_op jit(solution)/shard_map/all_gather | solution.py:30
  59.9 0.6 gather_fusion
  60.5 0.1 broadcast_select_fusion
  60.6 162.0 %all_gather.6 = bf16[4096,64]{1,0:T(8,128)(2,1)S(1)} all-gather(bf16[64,64]{1,0:T(8,128)(2,1)S(1)} %broadcast_select_fusion), channel_id=1, replica_groups=mesh['blk'=8,'stripe'=64] {'stripe'}, dimensions={0}, use_global_device_ids=true | all-gather | bytes 532480 | tf_op jit(solution)/shard_map/all_gather | solution.py:54
  222.5 0.6 multiply_reduce_fusion.2
  223.2 0.8 gather_fusion.1
  224.6 0.0 copy-done
  224.6 0.8 gather_fusion.2
  225.4 0.5 copy.13
  225.9 1.3 dynamic-slice
  227.8 0.0 all-to-all-done
  227.9 0.0 copy-start.3
  227.9 0.0 copy-start.1
  227.9 0.0 copy-start.2
  227.9 49.7 %while.11 = (s32[]{:T(128)}, f32[4096]{0:T(1024)S(1)}, f32[4096]{0:T(1024)S(1)}, bf16[8,512,64]{2,1,0:T(8,128)(2,1)S(1)}, bf16[4096,64]{1,0:T(8,128)(2,1)S(1)}, /*index=5*/f32[8,512]{1,0:T(8,128)S(1)}, s32[]{:T(128)}, s32[]{:T(128)}) while((s32[]{:T(128)}, f32[4096]{0:T(1024)S(1)}, f32[4096]{0:T(1024)S(1)}, ...), condition=%wide.region_4.5_spmd.clone, body=%wide.region_1.0_spmd.clone.sunk | while | flops 289508864 | bytes 1337459 | solution.py:42
  227.9 0.2 multiply_reduce_fusion.5
  228.1 6.0 multiply_reduce_fusion.6
  234.1 0.2 multiply_reduce_fusion.5
  234.3 6.0 multiply_reduce_fusion.6
  240.3 0.2 multiply_reduce_fusion.5
  240.5 6.0 multiply_reduce_fusion.6
  246.5 0.2 multiply_reduce_fusion.5
  246.7 6.0 multiply_reduce_fusion.6
  252.8 0.2 multiply_reduce_fusion.5
  252.9 6.0 multiply_reduce_fusion.6
  259.0 0.2 multiply_reduce_fusion.5
  259.1 6.0 multiply_reduce_fusion.6
  265.2 0.2 multiply_reduce_fusion.5
  265.3 6.0 multiply_reduce_fusion.6
  271.4 0.2 multiply_reduce_fusion.5
  271.5 6.0 multiply_reduce_fusion.6
  277.6 556.0 %all-reduce = f32[4096]{0:T(1024)S(1)} all-reduce(f32[4096]{0:T(1024)S(1)} %get-tuple-element.35), channel_id=2, replica_groups=mesh['blk'=8,'stripe'=64] {'stripe'}, use_global_device_ids=true, to_apply=%region_5.6.clone | all-reduce | flops 4096 | bytes 32768
  833.5 0.0 copy-done.3
  833.5 0.2 fusion.6
  833.8 0.0 copy-done.1
  833.8 0.0 copy-done.2
  833.8 0.6 fusion.21
  (19 shorter events, 0.1 us)
Async XLA Ops:
  0.6 224.0 %copy-start = (f32[512]{0:T(512)S(1)}, f32[512]{0:T(512)}, u32[]{:S(2)}) copy-start(f32[512]{0:T(512)} %param.13) | copy-start | bytes 6148
  2.0 225.9 %all-to-all-start = ((f32[8,1,512]{2,1,0:T(1,128)}), f32[8,1,512]{2,1,0:T(1,128)S(1)}, u32[]{:S(2)}, u32[]{:S(2)}) async-start(f32[8,1,512]{2,1,0:T(1,128)} %stack.2), calls=%async_computation | async-start | bytes 32768 | tf_op jit(solution)/shard_map/all_to_all | solution.py:27
  227.9 605.7 %copy-start.3 = (s32[64]{0:T(128)S(1)}, s32[64]{0:T(128)}, u32[]{:S(2)}) copy-start(s32[64]{0:T(128)} %param.14) | copy-start | bytes 772
  227.9 605.9 %copy-start.1 = (f32[512]{0:T(512)S(1)}, f32[512]{0:T(512)}, u32[]{:S(2)}) copy-start(f32[512]{0:T(512)} %param.11) | copy-start | bytes 6148
  227.9 605.9 %copy-start.2 = (f32[512]{0:T(512)S(1)}, f32[512]{0:T(512)}, u32[]{:S(2)}) copy-start(f32[512]{0:T(512)} %param.12) | copy-start | bytes 6148
